TPU v7x, 512 devices: a whole 4x8x8 slice. The times are simulated.
512 devices in a mesh: ep: 16 (over y, core), tp: 32 (over z, x).
Axes of the slice: x: 4, y: 8, z: 8, core: 2. Of those that a mesh axis runs over, the one named last changes fastest.
Arguments:
- attn_out: bfloat16 [2048, 2048], P('ep'), may hold values from -6 to 6
- residual_in: bfloat16 [2048, 2048], P('ep'), may hold values from -6 to 6
- w_out: bfloat16 [2048, 2048], P(None, 'tp'), may hold values from -0.125 to 0.125
- gain_in: float32 [2048], replicated, may hold values from 0.1 to 1.9
- router_logits: float32 [2048, 8], P('ep'), may hold values from -8 to 8
- expert_ids: int32 [2048, 2], P('ep'), may hold values from 0 to 7, all different within a row; in each aligned block of 128 rows (0 to 127, 128 to 255, ...) at most 64 rows name the same one
- copy_of: int32 [16, 8], replicated, may hold values from 0 to 15, as said below
- w_gate: bfloat16 [16, 2048, 5632], P('ep', None, 'tp')
- w_up: bfloat16 [16, 2048, 5632], P('ep', None, 'tp')
- w_down: bfloat16 [16, 5632, 2048], P('ep', 'tp')
- gain_out: float32 [2048], replicated, may hold values from 0.1 to 1.9
Outputs:
- layer_out: bfloat16 [2048, 2048], P(('ep', 'tp'))
- next_input: bfloat16 [2048, 2048], P(('ep', 'tp'))
Inputs may be any that keep to these rules, and one draw needn't show every extreme that they name: `expert_ids`: each row names 2 different experts. Within the rows of one ep group (aligned blocks of 128 rows) no expert is named by more than 64 rows, and in every draw some group has an expert named by exactly 64 rows. copy_of[s, e] is a copy of expert e, so different experts of one group go to different copies; copies of one expert carry equal weights.
All inputs are finite; a program needn't handle non-finite values.
Results may differ from a plain program's by a relative error of at most 0.019.
Values may be sent and summed in bfloat16 or wider, within the bound.
A program may use at most 64 MiB of HBM per device.

v0:
```python
import jax
import jax.numpy as jnp
from jax import lax
from jax.sharding import PartitionSpec as P


def rms_scale(values, gain):
    mean_square = jnp.mean(values * values, axis=-1, keepdims=True)
    return values * lax.rsqrt(mean_square + 1e-06) * gain


def expert_terms(slots, gate_weight, up_weight, down_weight):
    gate_value = jnp.einsum(
        "scmd,cdf->scmf", slots, gate_weight, preferred_element_type=jnp.float32
    )
    up_value = jnp.einsum("scmd,cdf->scmf", slots, up_weight, preferred_element_type=jnp.float32)
    hidden = (jax.nn.silu(gate_value) * up_value).astype(jnp.bfloat16)
    return jnp.einsum("scmf,cfd->scmd", hidden, down_weight, preferred_element_type=jnp.float32)


def per_device(
    attn_out,
    residual_in,
    w_out,
    gain_in,
    router_logits,
    expert_ids,
    copy_of,
    w_gate,
    w_up,
    w_down,
    gain_out,
):
    group_rows = attn_out.shape[0]
    model_width = attn_out.shape[1]
    tp_count = lax.axis_size("tp")
    ep_count = lax.axis_size("ep")
    own_rows = group_rows // tp_count
    capacity = group_rows // 2
    copies_here = w_gate.shape[0]
    copies_all = copies_here * ep_count
    experts_all = router_logits.shape[1]
    group_index = lax.axis_index("ep")
    tp_index = lax.axis_index("tp")
    columns = jnp.dot(attn_out, w_out, preferred_element_type=jnp.float32).astype(jnp.bfloat16)
    projected = lax.all_gather(columns, "tp", axis=1, tiled=True)
    carried = (residual_in.astype(jnp.float32) + projected.astype(jnp.float32)).astype(jnp.bfloat16)
    normed = rms_scale(carried.astype(jnp.float32), gain_in).astype(jnp.bfloat16)
    expert_grid = jnp.arange(experts_all, dtype=jnp.int32)
    picked = expert_ids[:, :, None] == expert_grid[None, None, :]
    chosen = jnp.sum(jnp.where(picked, router_logits[:, None, :], 0.0), axis=2)
    gate_share = jax.nn.sigmoid(chosen - chosen[:, ::-1])
    group_copies = lax.dynamic_slice_in_dim(copy_of, group_index, 1, 0)[0]
    target = jnp.sum(jnp.where(picked, group_copies[None, None, :], 0), axis=2)
    copy_hits = (
        target[:, :, None] == jnp.arange(copies_all, dtype=jnp.int32)[None, None, :]
    ).astype(jnp.int32)
    per_row = jnp.sum(copy_hits, axis=1)
    before = jnp.cumsum(per_row, axis=0) - per_row
    position = jnp.sum(copy_hits * before[:, None, :], axis=2)
    slot_index = target * capacity + position
    row_numbers = jnp.broadcast_to(
        jnp.arange(group_rows, dtype=jnp.int32)[:, None], slot_index.shape
    )
    slot_rows = (
        jnp.zeros((copies_all * capacity,), jnp.int32)
        .at[slot_index.reshape(-1)]
        .set(row_numbers.reshape(-1))
    )
    rows_table = slot_rows.reshape(ep_count, copies_here, capacity)
    outgoing = jnp.take(normed, rows_table, axis=0)
    arrived = lax.all_to_all(outgoing, "ep", split_axis=0, concat_axis=0, tiled=True)
    partial_value = expert_terms(arrived, w_gate, w_up, w_down)
    summed = lax.psum_scatter(
        partial_value.astype(jnp.bfloat16), "tp", scatter_dimension=2, tiled=True
    )
    returned = lax.all_to_all(summed, "ep", split_axis=0, concat_axis=0, tiled=True)
    own_target = lax.dynamic_slice_in_dim(target, tp_index * own_rows, own_rows, 0)
    own_position = lax.dynamic_slice_in_dim(position, tp_index * own_rows, own_rows, 0)
    own_gates = lax.dynamic_slice_in_dim(gate_share, tp_index * own_rows, own_rows, 0)
    portion = lax.all_gather(returned, "tp", axis=2, tiled=True)
    span_rows = portion.shape[2]
    flat_portion = portion.reshape(copies_all, span_rows, model_width)
    inside = (own_position >= 0) & (own_position < span_rows)
    picked_rows = flat_portion[own_target, jnp.clip(own_position, 0, span_rows - 1)]
    row_weights = jnp.where(inside, own_gates, 0.0)
    mixture = jnp.sum(row_weights[:, :, None] * picked_rows.astype(jnp.float32), axis=1)
    own_carried = lax.dynamic_slice_in_dim(carried, tp_index * own_rows, own_rows, 0)
    layer_out = (own_carried.astype(jnp.float32) + mixture).astype(jnp.bfloat16)
    next_input = rms_scale(layer_out.astype(jnp.float32), gain_out).astype(jnp.bfloat16)
    return (layer_out, next_input)


def solution(mesh):
    return jax.shard_map(
        per_device,
        mesh=mesh,
        in_specs=(
            P("ep", None),
            P("ep", None),
            P(None, "tp"),
            P(),
            P("ep", None),
            P("ep", None),
            P(),
            P("ep", None, "tp"),
            P("ep", None, "tp"),
            P("ep", "tp", None),
            P(),
        ),
        out_specs=(P(("ep", "tp"), None), P(("ep", "tp"), None)),
        check_vma=False,
    )
```

profile of v0, /device:TPU:8, one launch (start us, length us, event | category | flops | bytes accessed | tf_op | source)
XLA Modules:
  0.0 536.4 jit_solution(7059032426642041962)
XLA Ops:
  7.2 0.9 dynamic-slice_reduce_fusion
  8.2 0.8 select_reduce_fusion.2
  9.0 0.2 reduce_window_sum.11
  9.8 1.4 scatter_custom_fusion
  11.4 1.4 convolution_convert_fusion
  12.8 55.7 %all_gather.6 = bf16[128,2048]{0,1:T(8,128)(2,1)S(1)} all-gather(bf16[128,64]{0,1:T(8,128)(2,1)S(1)} %convolution_convert_fusion), channel_id=1, replica_groups=mesh['ep'=16,'tp'=32] {'tp'}, dimensions={1}, use_global_device_ids=true | all-gather | bytes 540672 | tf_op jit(solution)/shard_map/all_gather | solution.py:46
  68.5 0.2 copy.67
  68.7 1.3 fusion.19
  70.0 0.2 fusion.21
  70.2 6.0 %gather_fusion = bf16[1024,2048]{1,0:T(8,128)(2,1)} fusion(bf16[128,2048]{1,0:T(8,128)(2,1)S(1)} %fusion.21, s32[1024]{0:T(1024)S(1)} %broadcast_clamp_fusion), kind=kCustom, calls=%fused_computation | custom fusion | bytes 8392704 | tf_op jit(solution)/shard_map/jit(_take)/gather | solution.py:71
  76.3 2.6 broadcast_select_fusion
  78.9 100.5 %all_to_all.10 = bf16[16,1,64,2048]{3,2,1,0:T(8,128)(2,1)S(1)} all-to-all(bf16[16,1,64,2048]{3,2,1,0:T(8,128)(2,1)S(1)} %broadcast_select_fusion), channel_id=1, replica_groups=mesh['ep'=16,'tp'=32] {'ep'}, dimensions={0} | all-to-all | bytes 8388608 | tf_op jit(solution)/shard_map/all_to_all | solution.py:72
  179.4 2.0 copy-done.1
  181.4 2.3 fusion.4
  183.7 8.8 %convert_bitcast_fusion = bf16[16,1,64,2048]{3,2,0,1:T(8,128)(2,1)} fusion(bf16[16,1,64,2048]{3,2,1,0:T(8,128)(2,1)} %copy-done.1, f32[16,1,64,176]{3,2,0,1:T(8,128)} %fusion.4, bf16[1,176,2048]{2,1,0:T(8,128)(2,1)S(1)} %copy-done, bf16[1,2048,176]{1,2,0:T(8,128)(2,1)S(1)} %copy-done.8), kind=kOutput, calls=%fused_computation.8 | convolution fusion | flops 1479573504 | bytes 10551296 | tf_op jit(solution)/shard_map/scmf,cfd->scmd/dot_general | solution.py:18
  192.5 6.5 %copy.74 = bf16[16,1,64,2048]{3,0,1,2:T(8,128)(2,1)} copy(bf16[16,1,64,2048]{3,2,0,1:T(8,128)(2,1)} %convert_bitcast_fusion) | data formatting | bytes 8388608 | tf_op jit(solution)/shard_map/convert_element_type | solution.py:75
  199.0 221.9 %reduce-scatter.2.cloned.1.call-done = bf16[16,1,2,2048]{3,0,1,2:T(8,128)(2,1)} async-done(((bf16[16,1,64,2048]{3,0,1,2:T(8,128)(2,1)}), bf16[16,1,2,2048]{3,0,1,2:T(8,128)(2,1)}) %reduce-scatter.2.cloned.1.call-update) | async-done | bytes 131088 | tf_op jit(solution)/shard_map/reduce_scatter | solution.py:74
  420.9 1.0 copy.75
  422.0 14.5 %all_to_all.11 = bf16[16,1,2,2048]{3,2,1,0:T(2,128)(2,1)S(1)} all-to-all(bf16[16,1,2,2048]{3,2,1,0:T(2,128)(2,1)S(1)} %copy.75), channel_id=1, replica_groups=mesh['ep'=16,'tp'=32] {'ep'}, dimensions={0} | all-to-all | bytes 262144 | tf_op jit(solution)/shard_map/all_to_all | solution.py:77
  436.5 0.7 copy.76
  437.7 82.9 %all-gather.2.cloned.1.call-done = bf16[16,1,64,2048]{3,0,1,2:T(8,128)(2,1)} async-done(((bf16[16,1,2,2048]{3,0,1,2:T(8,128)(2,1)}), bf16[16,1,64,2048]{3,0,1,2:T(8,128)(2,1)}) %all-gather.2.cloned.1.call-update) | async-done | bytes 4194320 | tf_op jit(solution)/shard_map/all_gather | solution.py:81
  520.6 6.5 %copy.80 = bf16[16,1,64,2048]{3,2,0,1:T(8,128)(2,1)} copy(bf16[16,1,64,2048]{3,0,1,2:T(8,128)(2,1)} %all-gather.2.cloned.1.call-done) | data formatting | bytes 8388608 | tf_op jit(solution)/shard_map/all_gather | solution.py:81
  527.0 1.4 gather_fusion.1
  528.8 0.7 fusion.31
  (51 shorter events, 1.8 us)
Async XLA Ops:
  7.2 176.5 %copy-start = (bf16[1,176,2048]{2,1,0:T(8,128)(2,1)S(1)}, bf16[1,176,2048]{2,1,0:T(8,128)(2,1)}, u32[]{:S(2)}) copy-start(bf16[1,176,2048]{2,1,0:T(8,128)(2,1)} %param.20) | copy-start | bytes 2162692
  7.2 62.8 %copy-start.3 = (f32[2048]{0:T(1024)S(1)}, f32[2048]{0:T(1024)}, u32[]{:S(2)}) copy-start(f32[2048]{0:T(1024)} %param.14) | copy-start | bytes 24580
  7.2 413.7 %reduce-scatter.2.cloned.1.call-start = ((), (), s32[]{:S(2)}) async-start(), calls=%async_computation.3 | async-start | bytes 4325376 | tf_op jit(solution)/shard_map/reduce_scatter | solution.py:74
  78.9 102.5 %copy-start.7 = (bf16[1,2048,176]{1,2,0:T(8,128)(2,1)S(1)}, bf16[1,2048,176]{1,2,0:T(8,128)(2,1)}, u32[]{:S(2)}) copy-start(bf16[1,2048,176]{1,2,0:T(8,128)(2,1)} %param.18) | copy-start | bytes 2162692
  179.4 2.0 copy-start.1
  181.4 2.3 copy-start.8
  198.9 238.6 %copy-start.5 = (f32[128,8]{0,1:T(8,128)S(1)}, f32[128,8]{0,1:T(8,128)}, u32[]{:S(2)}) copy-start(f32[128,8]{0,1:T(8,128)} %param.15) | copy-start | bytes 12292
  198.9 238.6 %copy-start.6 = (s32[128,2]{0,1:T(2,128)S(1)}, s32[128,2]{0,1:T(2,128)}, u32[]{:S(2)}) copy-start(s32[128,2]{0,1:T(2,128)} %param.16) | copy-start | bytes 3076
  199.0 321.6 %all-gather.2.cloned.1.call-start = ((), (), s32[]{:S(2)}) async-start(), calls=%async_computation.4 | async-start | bytes 4325376 | tf_op jit(solution)/shard_map/all_gather | solution.py:81
  437.7 91.1 %copy-start.4 = (f32[2048]{0:T(1024)S(1)}, f32[2048]{0:T(1024)}, u32[]{:S(2)}) copy-start(f32[2048]{0:T(1024)} %param.21) | copy-start | bytes 24580
  528.8 0.7 copy-start.2
Sparse Core Ops, SparseCore 0:
  199.1 221.8 reduce-scatter.1
  437.3 83.1 all-gather.1
where the time goes:
time: 537 us; the launch traced here: 536 us
  waiting for transfers between devices  305 us (57%)
  blocking collectives  171 us (32%)
  local copies, waits for them, and re-layouts  27.7 us (5%)
  between operations  14.2 us (3%)
  matrix products  12.5 us (2%)
  other arithmetic  6.33 us (1%)
    reduce_scatter x1, waiting for transfers between devices, per_device(): lax.psum_scatter(partial_value.astype(jnp.bfloat16), 'tp', scatter_dimens...  222 us
    all_to_all x1, blocking collectives, per_device(): lax.all_to_all(outgoing, 'ep', split_axis=0, concat_axis=0, tiled=True)  100 us
    all_gather x1, waiting for transfers between devices, per_device(): portion = lax.all_gather(returned, 'tp', axis=2, tiled=True)  82.9 us
    all_gather x1, blocking collectives, per_device(): projected = lax.all_gather(columns, 'tp', axis=1, tiled=True)  55.7 us
    all_to_all x1, blocking collectives, per_device(): lax.all_to_all(summed, 'ep', split_axis=0, concat_axis=0, tiled=True)  14.5 us
  transfers between devices with their start and end apart: 2, of which 2 were waited for; matrix products, arithmetic and copies ran while one was open for 0% of the time, Pallas kernels for 0%

commit v1 on v0

--- a/solution.py
+++ b/solution.py
@@ -43,7 +43,9 @@
     group_index = lax.axis_index("ep")
     tp_index = lax.axis_index("tp")
     columns = jnp.dot(attn_out, w_out, preferred_element_type=jnp.float32).astype(jnp.bfloat16)
-    projected = lax.all_gather(columns, "tp", axis=1, tiled=True)
+    projected = jnp.concatenate(
+        lax.all_to_all(jnp.stack(lax.psum(1, "tp") * [columns]), "tp", 0, 0), axis=1
+    )
     carried = (residual_in.astype(jnp.float32) + projected.astype(jnp.float32)).astype(jnp.bfloat16)
     normed = rms_scale(carried.astype(jnp.float32), gain_in).astype(jnp.bfloat16)
     expert_grid = jnp.arange(experts_all, dtype=jnp.int32)

time: 537 us -> 508 us (0.946)
  blocking collectives: 171 us -> 115 us
  starting transfers between devices: 0.08 us -> 13.2 us
  waiting for transfers between devices: 305 us -> 318 us
    all_gather x1 -> x0, blocking collectives: 55.7 us -> none  [per_device(): projected = lax.all_gather(columns, 'tp', axis=1, tiled=True)]
    all_to_all x0 -> x1, waiting for transfers between devices: none -> 13.5 us  [per_device(): lax.all_to_all(jnp.stack(lax.psum(1, 'tp') * [columns]), 'tp', 0, 0)]
    all_to_all x0 -> x1, starting transfers between devices: none -> 13.2 us  [per_device(): lax.all_to_all(jnp.stack(lax.psum(1, 'tp') * [columns]), 'tp', 0, 0)]
  transfers between devices with their start and end apart: 2 -> 3, of which waited for: 2 -> 3; matrix products, arithmetic and copies ran while one was open for 0% -> 1% of each run, Pallas kernels for 0% -> 0%
where the time goes in v1:
time: 508 us; the launch traced here: 507 us
  waiting for transfers between devices  318 us (63%)
  blocking collectives  115 us (23%)
  local copies, waits for them, and re-layouts  28.7 us (6%)
  between operations  14.2 us (3%)
  starting transfers between devices  13.2 us (3%)
  matrix products  12.6 us (2%)
  other arithmetic  5.36 us (1%)
    reduce_scatter x1, waiting for transfers between devices, per_device(): lax.psum_scatter(partial_value.astype(jnp.bfloat16), 'tp', scatter_dimens...  222 us
    all_to_all x1, blocking collectives, per_device(): lax.all_to_all(outgoing, 'ep', split_axis=0, concat_axis=0, tiled=True)  100 us
    all_gather x1, waiting for transfers between devices, per_device(): portion = lax.all_gather(returned, 'tp', axis=2, tiled=True)  83 us
    all_to_all x1, blocking collectives, per_device(): lax.all_to_all(summed, 'ep', split_axis=0, concat_axis=0, tiled=True)  14.5 us
    all_to_all x1, waiting for transfers between devices, per_device(): lax.all_to_all(jnp.stack(lax.psum(1, 'tp') * [columns]), 'tp', 0, 0)  13.5 us
    all_to_all x1, starting transfers between devices, per_device(): lax.all_to_all(jnp.stack(lax.psum(1, 'tp') * [columns]), 'tp', 0, 0)  13.2 us
  transfers between devices with their start and end apart: 3, of which 3 were waited for; matrix products, arithmetic and copies ran while one was open for 1% of the time, Pallas kernels for 0%

profile of v1, /device:TPU:8, one launch (start us, length us, event | category | flops | bytes accessed | tf_op | source)
XLA Modules:
  0.0 507.4 jit_solution(17217444996815037729)
XLA Ops:
  7.2 1.5 convolution_convert_fusion
  8.7 0.9 stack.2
  9.6 13.2 %all-to-all-start = ((bf16[32,128,64]{1,2,0:T(8,128)(2,1)}), bf16[32,128,64]{1,2,0:T(8,128)(2,1)S(1)}, u32[]{:S(2)}, u32[]{:S(2)}) async-start(bf16[32,128,64]{1,2,0:T(8,128)(2,1)} %stack.2), calls=%async_computation | async-start | bytes 1048576 | tf_op jit(solution)/shard_map/all_to_all | solution.py:47
  22.8 0.9 dynamic-slice_reduce_fusion
  23.7 0.8 select_reduce_fusion.2
  25.3 1.4 scatter_custom_fusion
  27.0 13.5 %all-to-all-done = bf16[32,128,64]{1,2,0:T(8,128)(2,1)S(1)} async-done(((bf16[32,128,64]{1,2,0:T(8,128)(2,1)}), bf16[32,128,64]{1,2,0:T(8,128)(2,1)S(1)}, u32[]{:S(2)}, u32[]{:S(2)}) %all-to-all-start) | async-done | bytes 524320 | tf_op jit(solution)/shard_map/all_to_all | solution.py:47
  40.6 0.3 copy.27
  41.0 0.2 fusion.19
  41.4 6.0 %gather_fusion = bf16[1024,2048]{1,0:T(8,128)(2,1)} fusion(bf16[128,2048]{1,0:T(8,128)(2,1)S(1)} %fusion.21, s32[1024]{0:T(1024)S(1)} %broadcast_clamp_fusion), kind=kCustom, calls=%fused_computation | custom fusion | bytes 8392704 | tf_op jit(solution)/shard_map/jit(_take)/gather | solution.py:73
  47.4 2.6 broadcast_select_fusion
  50.1 100.5 %all_to_all.15 = bf16[16,1,64,2048]{3,2,1,0:T(8,128)(2,1)S(1)} all-to-all(bf16[16,1,64,2048]{3,2,1,0:T(8,128)(2,1)S(1)} %broadcast_select_fusion), channel_id=1, replica_groups=mesh['ep'=16,'tp'=32] {'ep'}, dimensions={0} | all-to-all | bytes 8388608 | tf_op jit(solution)/shard_map/all_to_all | solution.py:74
  150.6 2.0 copy-done.1
  152.6 2.3 fusion.4
  154.9 8.8 %convert_bitcast_fusion = bf16[16,1,64,2048]{3,2,0,1:T(8,128)(2,1)} fusion(bf16[16,1,64,2048]{3,2,1,0:T(8,128)(2,1)} %copy-done.1, f32[16,1,64,176]{3,2,0,1:T(8,128)} %fusion.4, bf16[1,176,2048]{2,1,0:T(8,128)(2,1)S(1)} %copy-done, bf16[1,2048,176]{1,2,0:T(8,128)(2,1)S(1)} %copy-done.9), kind=kOutput, calls=%fused_computation.8 | convolution fusion | flops 1479573504 | bytes 10551296 | tf_op jit(solution)/shard_map/scmf,cfd->scmd/dot_general | solution.py:18
  163.7 6.5 %copy.34 = bf16[16,1,64,2048]{3,0,1,2:T(8,128)(2,1)} copy(bf16[16,1,64,2048]{3,2,0,1:T(8,128)(2,1)} %convert_bitcast_fusion) | data formatting | bytes 8388608 | tf_op jit(solution)/shard_map/convert_element_type | solution.py:77
  170.2 221.6 %reduce-scatter.2.cloned.1.call-done = bf16[16,1,2,2048]{3,0,1,2:T(8,128)(2,1)} async-done(((bf16[16,1,64,2048]{3,0,1,2:T(8,128)(2,1)}), bf16[16,1,2,2048]{3,0,1,2:T(8,128)(2,1)}) %reduce-scatter.2.cloned.1.call-update) | async-done | bytes 131088 | tf_op jit(solution)/shard_map/reduce_scatter | solution.py:76
  391.9 1.0 copy.35
  392.9 14.5 %all_to_all.16 = bf16[16,1,2,2048]{3,2,1,0:T(2,128)(2,1)S(1)} all-to-all(bf16[16,1,2,2048]{3,2,1,0:T(2,128)(2,1)S(1)} %copy.35), channel_id=1, replica_groups=mesh['ep'=16,'tp'=32] {'ep'}, dimensions={0} | all-to-all | bytes 262144 | tf_op jit(solution)/shard_map/all_to_all | solution.py:79
  407.4 0.7 copy.36
  408.6 83.0 %all-gather.2.cloned.1.call-done = bf16[16,1,64,2048]{3,0,1,2:T(8,128)(2,1)} async-done(((bf16[16,1,2,2048]{3,0,1,2:T(8,128)(2,1)}), bf16[16,1,64,2048]{3,0,1,2:T(8,128)(2,1)}) %all-gather.2.cloned.1.call-update) | async-done | bytes 4194320 | tf_op jit(solution)/shard_map/all_gather | solution.py:83
  491.6 6.5 %copy.40 = bf16[16,1,64,2048]{3,2,0,1:T(8,128)(2,1)} copy(bf16[16,1,64,2048]{3,0,1,2:T(8,128)(2,1)} %all-gather.2.cloned.1.call-done) | data formatting | bytes 8388608 | tf_op jit(solution)/shard_map/all_gather | solution.py:83
  498.0 1.4 gather_fusion.1
  499.8 0.7 fusion.31
  (56 shorter events, 2.3 us)
Async XLA Ops:
  7.2 147.7 %copy-start = (bf16[1,176,2048]{2,1,0:T(8,128)(2,1)S(1)}, bf16[1,176,2048]{2,1,0:T(8,128)(2,1)}, u32[]{:S(2)}) copy-start(bf16[1,176,2048]{2,1,0:T(8,128)(2,1)} %param.20) | copy-start | bytes 2162692
  7.2 33.8 %copy-start.2 = (bf16[128,2048]{1,0:T(8,128)(2,1)S(1)}, bf16[128,2048]{1,0:T(8,128)(2,1)}, u32[]{:S(2)}) copy-start(bf16[128,2048]{1,0:T(8,128)(2,1)} %param.12) | copy-start | bytes 1572868
  8.7 32.5 %copy-start.4 = (f32[2048]{0:T(1024)S(1)}, f32[2048]{0:T(1024)}, u32[]{:S(2)}) copy-start(f32[2048]{0:T(1024)} %param.14) | copy-start | bytes 24580
  9.6 30.9 %all-to-all-start = ((bf16[32,128,64]{1,2,0:T(8,128)(2,1)}), bf16[32,128,64]{1,2,0:T(8,128)(2,1)S(1)}, u32[]{:S(2)}, u32[]{:S(2)}) async-start(bf16[32,128,64]{1,2,0:T(8,128)(2,1)} %stack.2), calls=%async_computation | async-start | bytes 1048576 | tf_op jit(solution)/shard_map/all_to_all | solution.py:47
  22.8 369.1 %reduce-scatter.2.cloned.1.call-start = ((), (), s32[]{:S(2)}) async-start(), calls=%async_computation.4 | async-start | bytes 4325376 | tf_op jit(solution)/shard_map/reduce_scatter | solution.py:76
  50.1 102.5 %copy-start.8 = (bf16[1,2048,176]{1,2,0:T(8,128)(2,1)S(1)}, bf16[1,2048,176]{1,2,0:T(8,128)(2,1)}, u32[]{:S(2)}) copy-start(bf16[1,2048,176]{1,2,0:T(8,128)(2,1)} %param.18) | copy-start | bytes 2162692
  150.6 2.0 copy-start.1
  152.6 2.3 copy-start.9
  170.1 238.2 %copy-start.6 = (f32[128,8]{0,1:T(8,128)S(1)}, f32[128,8]{0,1:T(8,128)}, u32[]{:S(2)}) copy-start(f32[128,8]{0,1:T(8,128)} %param.15) | copy-start | bytes 12292
  170.1 238.2 %copy-start.7 = (s32[128,2]{0,1:T(2,128)S(1)}, s32[128,2]{0,1:T(2,128)}, u32[]{:S(2)}) copy-start(s32[128,2]{0,1:T(2,128)} %param.16) | copy-start | bytes 3076
  170.2 321.4 %all-gather.2.cloned.1.call-start = ((), (), s32[]{:S(2)}) async-start(), calls=%async_computation.5 | async-start | bytes 4325376 | tf_op jit(solution)/shard_map/all_gather | solution.py:83
  408.6 91.2 %copy-start.5 = (f32[2048]{0:T(1024)S(1)}, f32[2048]{0:T(1024)}, u32[]{:S(2)}) copy-start(f32[2048]{0:T(1024)} %param.21) | copy-start | bytes 24580
  499.8 0.7 copy-start.3
Sparse Core Ops, SparseCore 0:
  170.3 221.5 reduce-scatter.1
  408.2 83.3 all-gather.1
